TPU v7x, 32 devices: a whole 2x2x4 slice. The times are simulated.
32 devices in a mesh: dp: 16 (over z, y, x), tensor: 2 (over core).
Axes of the slice: x: 2, y: 2, z: 4, core: 2. Of those that a mesh axis runs over, the one named last changes fastest.
Arguments:
- inputs: bfloat16 [25088, 512], P(('dp', 'tensor')), may hold values from -6 to 6
- cotangent: bfloat16 [25088, 512], P(('dp', 'tensor')), may hold values from -6 to 6
- region_ids: int32 [196], replicated, may hold values from 0 to 3
- rel_index: int32 [49, 49], replicated, may hold values from 0 to 168
- norm1_gain: bfloat16 [2, 512], replicated, may hold values from 0.5 to 1.5
- norm1_bias: bfloat16 [2, 512], replicated, may hold values from -1.75 to 1.75
- w_qkv: bfloat16 [2, 3, 512, 512], P(None, None, 'dp', 'tensor'), may hold values from -0.25 to 0.25
- qv_bias: bfloat16 [2, 2, 512], P(None, None, 'tensor'), may hold values from -1.75 to 1.75
- bias_table: bfloat16 [2, 16, 169], P(None, 'tensor'), may hold values from -3 to 250
- w_proj: bfloat16 [2, 512, 512], P(None, 'tensor', 'dp'), may hold values from -0.75 to 0.75
- proj_bias: bfloat16 [2, 512], replicated, may hold values from -1.75 to 1.75
- norm2_gain: bfloat16 [2, 512], replicated, may hold values from 0.5 to 1.5
- norm2_bias: bfloat16 [2, 512], replicated, may hold values from -1.75 to 1.75
- w_fc1: bfloat16 [2, 512, 2048], P(None, 'dp', 'tensor'), may hold values from -0.25 to 0.25
- fc1_bias: bfloat16 [2, 2048], P(None, 'tensor'), may hold values from -3 to 3
- w_fc2: bfloat16 [2, 2048, 512], P(None, 'tensor', 'dp'), may hold values from -0.125 to 0.125
- fc2_bias: bfloat16 [2, 512], replicated, may hold values from -1.75 to 1.75
Outputs:
- outputs: float32 [25088, 512], P(('dp', 'tensor'))
- input_grad: float32 [25088, 512], P(('dp', 'tensor'))
- norm1_gain_grad: float32 [2, 512], replicated
- norm1_bias_grad: float32 [2, 512], replicated
- w_qkv_grad: float32 [2, 3, 512, 512], P(None, None, 'dp', 'tensor')
- qv_bias_grad: float32 [2, 2, 512], P(None, None, 'tensor')
- bias_table_grad: float32 [2, 16, 169], P(None, 'tensor')
- w_proj_grad: float32 [2, 512, 512], P(None, 'tensor', 'dp')
- proj_bias_grad: float32 [2, 512], replicated
- norm2_gain_grad: float32 [2, 512], replicated
- norm2_bias_grad: float32 [2, 512], replicated
- w_fc1_grad: float32 [2, 512, 2048], P(None, 'dp', 'tensor')
- fc1_bias_grad: float32 [2, 2048], P(None, 'tensor')
- w_fc2_grad: float32 [2, 2048, 512], P(None, 'tensor', 'dp')
- fc2_bias_grad: float32 [2, 512], replicated
All inputs are finite; a program needn't handle non-finite values.
Results may differ from a plain program's by a relative error of at most 0.025.
Values may be sent and summed in bfloat16 or wider, within the bound.
A program may use at most 192 MiB of HBM per device.

v0:
```python
import functools
import itertools

import jax
import jax.numpy as jnp
from jax import lax
from jax.experimental import pallas as pl
from jax.experimental.pallas import tpu as pltpu
from jax.sharding import PartitionSpec as P

HD = 32
GRID = 14
WIN = 7
SHIFT = 3
LAYERS = 2
TABLE = 169
EPS = 1e-05
MASKED = -100.0
PADDED = -1e30
SLOT = 64
PER_STEP = 2
LANES = 128
EXACT_PRECISION = lax.Precision.HIGHEST
F32 = jnp.float32
BF16 = jnp.bfloat16


def normalize(residual):
    average = jnp.mean(residual, -1, keepdims=True)
    centered = residual - average
    inverse = lax.rsqrt(jnp.mean(centered * centered, -1, keepdims=True) + EPS)
    return (centered * inverse, inverse)


def norm_back(grad_out, normed, inverse, gain_value):
    scaled = grad_out * gain_value
    return inverse * (
        scaled
        - jnp.mean(scaled, -1, keepdims=True)
        - normed * jnp.mean(scaled * normed, -1, keepdims=True)
    )


def gelu_parts(hidden_pre):
    cumulative = 0.5 * (1.0 + lax.erf(hidden_pre * 0.7071067811865476))
    density = jnp.exp(-0.5 * hidden_pre * hidden_pre) * 0.3989422804014327
    return (hidden_pre * cumulative, cumulative + hidden_pre * density)


def dot(a, b, ca=1, cb=0):
    return lax.dot_general(a, b, (((ca,), (cb,)), ((), ())), preferred_element_type=F32)


def stack_heads(block, masks):
    return jnp.concatenate([block * m for m in masks], axis=0)


def merge_heads(stacked, masks):
    total = None
    for h, m in enumerate(masks):
        part = stacked[h * SLOT : (h + 1) * SLOT] * m
        total = part if total is None else total + part
    return total


def head_masks(dtype):
    lane = lax.broadcasted_iota(jnp.int32, (SLOT, LANES), 1)
    return [
        jnp.where((lane >= h * HD) & (lane < (h + 1) * HD), 1.0, 0.0).astype(dtype)
        for h in range(LANES // HD)
    ]


def probabilities(queries_stacked, keys, bias):
    scores = dot(queries_stacked, keys, 1, 1) + bias
    exponent = jnp.exp(scores - jnp.max(scores, -1, keepdims=True))
    return exponent * (1.0 / jnp.sum(exponent, -1, keepdims=True))


def attention_kernel(qkv_ref, bias_ref, mask_ref, out_ref):
    width = out_ref.shape[1]
    low, full = head_masks(BF16), head_masks(F32)
    for g, w in itertools.product(range(width // LANES), range(mask_ref.shape[0])):
        rows = slice(w * SLOT, (w + 1) * SLOT)
        mask = jnp.concatenate([mask_ref[w]] * len(low), axis=0)
        q = qkv_ref[rows, g * LANES : (g + 1) * LANES]
        k = qkv_ref[rows, width + g * LANES : width + (g + 1) * LANES]
        v = qkv_ref[rows, 2 * width + g * LANES : 2 * width + (g + 1) * LANES]
        attention = probabilities(stack_heads(q, low), k, bias_ref[g] + mask)
        mixed = dot(attention.astype(BF16), v)
        out_ref[rows, g * LANES : (g + 1) * LANES] = merge_heads(mixed, full).astype(BF16)


def attention_back_kernel(scale, qkv_ref, dmix_ref, bias_ref, mask_ref, dqkv_ref, dscore_ref, dbias_ref):
    width = dmix_ref.shape[1]
    low, full = head_masks(BF16), head_masks(F32)

    @pl.when(pl.program_id(0) == 0)
    def _():
        dscore_ref[...] = jnp.zeros_like(dscore_ref)
        dbias_ref[...] = jnp.zeros_like(dbias_ref)

    def put(part, g, at_rows, value):
        at = slice(part * width + g * LANES, part * width + (g + 1) * LANES)
        dqkv_ref[at_rows, at] = value.astype(BF16)
        if part != 1:
            rows = value[0:8]
            for r in range(1, SLOT // 8):
                rows = rows + value[r * 8 : (r + 1) * 8]
            dbias_ref[:, at] += rows

    for g, w in itertools.product(range(width // LANES), range(mask_ref.shape[0])):
        rows = slice(w * SLOT, (w + 1) * SLOT)
        mask = jnp.concatenate([mask_ref[w]] * len(low), axis=0)
        q = qkv_ref[rows, g * LANES : (g + 1) * LANES]
        k = qkv_ref[rows, width + g * LANES : width + (g + 1) * LANES]
        v = qkv_ref[rows, 2 * width + g * LANES : 2 * width + (g + 1) * LANES]
        dm = dmix_ref[rows, g * LANES : (g + 1) * LANES]
        q_stacked = stack_heads(q, low)
        dm_stacked = stack_heads(dm, low)
        attention = probabilities(q_stacked, k, bias_ref[g] + mask)
        dattention = dot(dm_stacked, v, 1, 1)
        inner = jnp.sum(attention * dattention, -1, keepdims=True)
        dscores = attention * (dattention - inner)
        dscore_ref[g] += dscores
        dl = dscores.astype(BF16)
        put(0, g, rows, merge_heads(dot(dl, k), full) * scale)
        put(1, g, rows, dot(dl, q_stacked, 0, 0))
        put(2, g, rows, dot(attention.astype(BF16), dm_stacked, 0, 0))


def attention_forward(qkv, bias, mask):
    rows, width = qkv.shape[0], qkv.shape[1] // 3
    windows = mask.shape[0]
    return pl.pallas_call(
        attention_kernel,
        grid=(rows // (PER_STEP * SLOT),),
        out_shape=jax.ShapeDtypeStruct((rows, width), BF16),
        in_specs=[
            pl.BlockSpec((PER_STEP * SLOT, 3 * width), lambda i: (i, 0)),
            pl.BlockSpec(bias.shape, lambda i: (0, 0, 0)),
            pl.BlockSpec((PER_STEP, SLOT, SLOT), lambda i: (lax.rem(i, windows // PER_STEP), 0, 0)),
        ],
        out_specs=pl.BlockSpec((PER_STEP * SLOT, width), lambda i: (i, 0)),
        cost_estimate=pl.CostEstimate(
            flops=rows * width * SLOT * 16, bytes_accessed=rows * width * 8, transcendentals=rows * width * 2
        ),
        name="attention_forward",
    )(qkv, bias, mask)


def attention_backward(qkv, dmix, bias, mask, scale):
    rows, width = dmix.shape
    windows = mask.shape[0]
    return pl.pallas_call(
        functools.partial(attention_back_kernel, scale),
        grid=(rows // (PER_STEP * SLOT),),
        out_shape=(
            jax.ShapeDtypeStruct((rows, 3 * width), BF16),
            jax.ShapeDtypeStruct(bias.shape, F32),
            jax.ShapeDtypeStruct((8, 3 * width), F32),
        ),
        in_specs=[
            pl.BlockSpec((PER_STEP * SLOT, 3 * width), lambda i: (i, 0)),
            pl.BlockSpec((PER_STEP * SLOT, width), lambda i: (i, 0)),
            pl.BlockSpec(bias.shape, lambda i: (0, 0, 0)),
            pl.BlockSpec((PER_STEP, SLOT, SLOT), lambda i: (lax.rem(i, windows // PER_STEP), 0, 0)),
        ],
        out_specs=(
            pl.BlockSpec((PER_STEP * SLOT, 3 * width), lambda i: (i, 0)),
            pl.BlockSpec(bias.shape, lambda i: (0, 0, 0)),
            pl.BlockSpec((8, 3 * width), lambda i: (0, 0)),
        ),
        cost_estimate=pl.CostEstimate(
            flops=rows * width * SLOT * 40, bytes_accessed=rows * width * 16, transcendentals=rows * width * 2
        ),
        name="attention_backward",
    )(qkv, dmix, bias, mask)


def placement(tokens, shift):
    per_side = GRID // WIN
    slots = tokens // (WIN * WIN) * SLOT
    row = lax.broadcasted_iota(jnp.int32, (slots, tokens), 0)
    column = lax.broadcasted_iota(jnp.int32, (slots, tokens), 1)
    window, p = row // SLOT, row % SLOT
    image, w = window // (per_side * per_side), window % (per_side * per_side)
    gi = (w // per_side * WIN + p // WIN + shift) % GRID
    gj = (w % per_side * WIN + p % WIN + shift) % GRID
    source = (
        image * (GRID * GRID)
        + (gi // WIN * per_side + gj // WIN) * (WIN * WIN)
        + gi % WIN * WIN
        + gj % WIN
    )
    return ((column == source) & (p < WIN * WIN)).astype(BF16)


def pack_weights(w_qkv, w_proj, w_fc1, w_fc2):
    rows = w_qkv.shape[1]
    return jnp.concatenate(
        [w_qkv.transpose(1, 0, 2).reshape(rows, -1), w_proj.T, w_fc1, w_fc2.T], axis=1
    )


def per_device(
    inputs,
    cotangent,
    region_ids,
    rel_index,
    norm1_gain,
    norm1_bias,
    w_qkv,
    qv_bias,
    bias_table,
    w_proj,
    proj_bias,
    norm2_gain,
    norm2_bias,
    w_fc1,
    fc1_bias,
    w_fc2,
    fc2_bias,
):
    n_dp, n_t = lax.axis_size("dp"), lax.axis_size("tensor")
    t_index = lax.axis_index("tensor")
    tokens, width = inputs.shape
    ff_local = fc1_bias.shape[1]
    heads_local = bias_table.shape[1]
    heads = heads_local * n_t
    local = heads_local * HD
    shard = width // n_dp
    cuts = (3 * local, 4 * local, 4 * local + ff_local, 4 * local + 2 * ff_local)
    per_side = GRID // WIN
    windows = per_side * per_side
    win_tokens = WIN * WIN
    score_scale = HD ** (-0.5)
    groups = width // LANES

    def pack_grads(g_qkv, g_proj, g_fc1, g_fc2):
        sides = []
        for t in range(n_t):
            pieces = []
            for g, n in ((g_qkv, 3), (g_proj, 1), (g_fc1, 1), (g_fc2, 1)):
                step = g.shape[1] // (n * n_t)
                pieces += [g[:, (m * n_t + t) * step : (m * n_t + t + 1) * step].astype(BF16) for m in range(n)]
            sides.append(jnp.concatenate(pieces, axis=1).reshape(n_dp, shard, -1))
        return jnp.stack(sides, axis=1)

    small = jnp.concatenate([qv_bias.reshape(-1), fc1_bias.reshape(-1), bias_table.reshape(-1)])
    extra = -(-small.shape[0] // (shard * LANES)) * LANES
    small_packed = jnp.pad(small, (0, shard * extra - small.shape[0])).reshape(shard, extra)

    def gather_layer(l):
        packed = pack_weights(w_qkv[l], w_proj[l], w_fc1[l], w_fc2[l])
        if l == 0:
            packed = jnp.concatenate([packed, small_packed], axis=1)
        whole = gather_shards(packed)
        return whole, whole[0, :, :, cuts[3] :].reshape(n_t, -1)

    def unpack_weights(whole):
        blocks = [whole[:, t].reshape(width, -1) for t in range(n_t)]
        parts = []
        lo = 0
        for n, hi in zip((3, 1, 1, 1), cuts):
            step = (hi - lo) // n
            parts.append(
                jnp.concatenate([b[:, lo + m * step : lo + (m + 1) * step] for m in range(n) for b in blocks], axis=1)
            )
            lo = hi
        return parts

    gathered = [gather_layer(l) for l in range(LAYERS)]
    wholes = [whole for whole, _ in gathered]
    weights = [None] * LAYERS
    small = gathered[0][1][:, : small.shape[0]]
    n_qv, n_fc = qv_bias.size, fc1_bias.size
    qv_full = small[:, :n_qv].reshape(n_t, LAYERS, 2, local).transpose(1, 2, 0, 3).reshape(LAYERS, 2, width)
    fc1_full = small[:, n_qv : n_qv + n_fc].reshape(n_t, LAYERS, ff_local).transpose(1, 0, 2).reshape(LAYERS, -1)
    table_full = (
        small[:, n_qv + n_fc :].reshape(n_t, LAYERS, heads_local, TABLE).transpose(1, 0, 2, 3).reshape(LAYERS, heads, TABLE)
    ).astype(F32)
    fc1_full = fc1_full.astype(F32)
    qv_full = qv_full.astype(F32)

    pad = SLOT - win_tokens
    index_padded = jnp.pad(rel_index, ((0, pad), (0, pad)), constant_values=-1).reshape(-1)
    one_hot = (index_padded[None, :] == jnp.arange(TABLE, dtype=jnp.int32)[:, None]).astype(F32)
    regions = region_ids.reshape(windows, win_tokens)
    shift_mask = jnp.where(regions[:, :, None] == regions[:, None, :], 0.0, MASKED).astype(F32)

    def padded_mask(mask):
        return jnp.pad(
            jnp.pad(mask, ((0, 0), (0, pad), (0, 0))), ((0, 0), (0, 0), (0, pad)), constant_values=PADDED
        )

    masks = [padded_mask(jnp.zeros_like(shift_mask)), padded_mask(shift_mask)]
    biases = [
        jnp.dot(table_full[l], one_hot, precision=EXACT_PRECISION).reshape(groups, LANES // HD * SLOT, SLOT)
        for l in range(LAYERS)
    ]
    places = [placement(tokens, SHIFT * (l % 2)) for l in range(LAYERS)]
    scale_row = jnp.concatenate([jnp.full((width,), score_scale, F32), jnp.ones((2 * width,), F32)])

    residual = inputs.astype(F32)
    store = []
    for l in range(LAYERS):
        whole, residual = lax.optimization_barrier((wholes[l], residual)) if l else (wholes[l], residual)
        weights[l] = unpack_weights(whole)
        qkv_w, proj_w, fc1_w, fc2_w = weights[l]
        place = places[l]
        normed1, inverse1 = normalize(residual)
        attn_in = (normed1 * norm1_gain[l].astype(F32) + norm1_bias[l].astype(F32)).astype(BF16)
        attn_pad = dot(place, attn_in).astype(BF16)
        qkv_bias = jnp.concatenate([qv_full[l, 0], jnp.zeros((width,), F32), qv_full[l, 1]])
        qkv = ((dot(attn_pad, qkv_w) + qkv_bias) * scale_row).astype(BF16)
        mixture = dot(place, attention_forward(qkv, biases[l], masks[l % 2]), 0, 0).astype(BF16)
        residual_mid = residual + dot(mixture, proj_w, 1, 1) + proj_bias[l].astype(F32)
        normed2, inverse2 = normalize(residual_mid)
        ffn_in = (normed2 * norm2_gain[l].astype(F32) + norm2_bias[l].astype(F32)).astype(BF16)
        activated, slope = gelu_parts(dot(ffn_in, fc1_w) + fc1_full[l])
        hidden = activated.astype(BF16)
        slope = slope.astype(BF16)
        store.append((normed1, inverse1, attn_in, qkv, mixture, normed2, inverse2, ffn_in, slope, hidden))
        residual = residual_mid + dot(hidden, fc2_w, 1, 1) + fc2_bias[l].astype(F32)

    g = cotangent.astype(F32)
    weight_grads = [None] * LAYERS
    small_grads = [None] * LAYERS
    for l in reversed(range(LAYERS)):
        qkv_w, proj_w, fc1_w, fc2_w = weights[l]
        place = places[l]
        normed1, inverse1, attn_in, qkv, mixture, normed2, inverse2, ffn_in, slope, hidden = store[l]
        g_fc2_bias = jnp.sum(g, 0)
        gl = g.astype(BF16)
        dpre = dot(gl, fc2_w) * slope.astype(F32)
        dpl = dpre.astype(BF16)
        g_fc1_bias = jnp.sum(dpre, 0)
        g_fc2 = dot(gl, hidden, 0, 0)
        g_fc1 = dot(ffn_in, dpl, 0, 0)
        dffn = dot(dpl, fc1_w, 1, 1)
        g_n2_gain = jnp.sum(dffn * normed2, 0)
        g_n2_bias = jnp.sum(dffn, 0)
        g_mid = g + norm_back(dffn, normed2, inverse2, norm2_gain[l].astype(F32))
        g_proj_bias = jnp.sum(g_mid, 0)
        gm = g_mid.astype(BF16)
        g_proj = dot(gm, mixture, 0, 0)
        dmix = dot(gm, proj_w).astype(BF16)
        dmix_pad = dot(place, dmix).astype(BF16)
        dqkv_pad, dscores, dbias = attention_backward(qkv, dmix_pad, biases[l], masks[l % 2], score_scale)
        g_table = lax.dot_general(
            dscores.reshape(heads, SLOT * SLOT), one_hot, (((1,), (1,)), ((), ())), precision=EXACT_PRECISION
        )
        dqkv = dot(place, dqkv_pad, 0, 0).astype(BF16)
        g_qkv = dot(attn_in, dqkv, 0, 0)
        dattn = dot(dqkv, qkv_w, 1, 1)
        g_n1_gain = jnp.sum(dattn * normed1, 0)
        g_n1_bias = jnp.sum(dattn, 0)
        g = g_mid + norm_back(dattn, normed1, inverse1, norm1_gain[l].astype(F32))
        dbias_rows = jnp.sum(dbias, 0)
        weight_grads[l] = reduce_shards(pack_grads(g_qkv, g_proj, g_fc1, g_fc2)).astype(F32)
        small_grads[l] = [
            g_n1_gain, g_n1_bias, g_proj_bias, g_n2_gain, g_n2_bias, g_fc2_bias,
            dbias_rows[:width], dbias_rows[2 * width :], g_fc1_bias, g_table.reshape(-1),
        ]

    flat = jnp.concatenate([v for l in range(LAYERS) for v in small_grads[l]])
    total = sum_everywhere(flat).reshape(LAYERS, -1)
    vectors = total[:, : 6 * width].reshape(LAYERS, 6, width)
    at = 6 * width
    qv_total = total[:, at : at + 2 * width].reshape(LAYERS, 2, width)
    qv_total = lax.dynamic_slice_in_dim(qv_total, t_index * local, local, 2)
    at += 2 * width
    fc1_total = lax.dynamic_slice_in_dim(total[:, at : at + ff_local * n_t], t_index * ff_local, ff_local, 1)
    at += ff_local * n_t
    table_total = lax.dynamic_slice_in_dim(
        total[:, at:].reshape(LAYERS, heads, TABLE), t_index * heads_local, heads_local, 1
    )
    grads = jnp.stack(weight_grads)
    qkv_total = grads[..., : cuts[0]].reshape(LAYERS, shard, 3, local).transpose(0, 2, 1, 3)
    proj_w_total = grads[..., cuts[0] : cuts[1]].transpose(0, 2, 1)
    fc1_w_total = grads[..., cuts[1] : cuts[2]]
    fc2_w_total = grads[..., cuts[2] :].transpose(0, 2, 1)
    return (
        residual,
        g,
        vectors[:, 0],
        vectors[:, 1],
        qkv_total,
        qv_total,
        table_total,
        proj_w_total,
        vectors[:, 2],
        vectors[:, 3],
        vectors[:, 4],
        fc1_w_total,
        fc1_total,
        fc2_w_total,
        vectors[:, 5],
    )


def gather_shards(packed):
    n_dp, n_t = lax.axis_size("dp"), lax.axis_size("tensor")
    rows = lax.all_gather(packed, ("dp", "tensor"), axis=0, tiled=False)
    return rows.reshape((n_dp, n_t) + packed.shape)


def reduce_shards(packed):
    rows = packed.reshape((-1,) + packed.shape[2:])
    return lax.psum_scatter(rows, ("dp", "tensor"), scatter_dimension=0, tiled=False)


def partners():
    found = []
    for axis in ("tensor", "dp"):
        size, bit = lax.axis_size(axis), 1
        assert size & (size - 1) == 0
        me = lax.axis_index(axis)
        while bit < size:
            found.append((axis, me + bit - 2 * bit * ((me // bit) % 2)))
            bit *= 2
    return found


def exchange_kernel(x_ref, out_ref, held, arrived, send_sem, recv_sem):
    steps = partners()
    barrier = pltpu.get_barrier_semaphore()
    for axis, place in steps:
        pl.semaphore_signal(barrier, inc=1, device_id={axis: place}, device_id_type=pl.DeviceIdType.MESH)
    pl.semaphore_wait(barrier, len(steps))
    for s, (axis, place) in enumerate(steps):
        source = x_ref if s == 0 else held.at[s - 1]
        copy = pltpu.make_async_remote_copy(
            src_ref=source,
            dst_ref=arrived.at[s],
            send_sem=send_sem.at[s],
            recv_sem=recv_sem.at[s],
            device_id={axis: place},
            device_id_type=pl.DeviceIdType.MESH,
        )
        copy.start()
        copy.wait()
        total = source[...] + arrived[s]
        if s < len(steps) - 1:
            held[s] = total
        else:
            out_ref[...] = total


def sum_everywhere(flat):
    size = flat.shape[0]
    rows = -(-size // (8 * LANES)) * 8
    x = jnp.pad(flat, (0, rows * LANES - size)).reshape(rows, LANES)
    n = len(partners())
    total = pl.pallas_call(
        exchange_kernel,
        out_shape=jax.ShapeDtypeStruct(x.shape, F32),
        in_specs=[pl.BlockSpec(memory_space=pltpu.VMEM)],
        out_specs=pl.BlockSpec(memory_space=pltpu.VMEM),
        scratch_shapes=[
            pltpu.VMEM((n,) + x.shape, F32),
            pltpu.VMEM((n,) + x.shape, F32),
            pltpu.SemaphoreType.DMA((n,)),
            pltpu.SemaphoreType.DMA((n,)),
        ],
        compiler_params=pltpu.CompilerParams(collective_id=0, has_side_effects=True),
        name="sum_everywhere",
    )(x)
    return total.reshape(-1)[:size]


SMALL_ROWS = 24
TABLE_LANES = 256
PARAMS = ("n1g", "n1b", "pb", "n2g", "n2b", "f2b")


def flip(index, bit):
    return index + bit - 2 * bit * ((index // bit) % 2)


def mix(index, j):
    bit = 1
    while bit <= j:
        if j & bit:
            index = flip(index, bit)
        bit *= 2
    return index


def shift_segments(shift):
    per_side = GRID // WIN
    moves = []
    for w in range(per_side * per_side):
        for p in range(WIN * WIN):
            gi = (w // per_side * WIN + p // WIN + shift) % GRID
            gj = (w % per_side * WIN + p % WIN + shift) % GRID
            source = (gi // WIN * per_side + gj // WIN) * SLOT + gi % WIN * WIN + gj % WIN
            moves.append((w * SLOT + p, source))
    runs = []
    for target, source in moves:
        if runs and runs[-1][0] + runs[-1][2] == target and runs[-1][1] + runs[-1][2] == source:
            runs[-1][2] += 1
        else:
            runs.append([target, source, 1])
    return runs


class Plan:
    def __init__(self, n_dp, tokens, width, ff_local, heads_local):
        self.Y = self.X = 2
        self.Z = n_dp // 4
        self.T = 2
        self.width = width
        self.shard = width // n_dp
        self.local = heads_local * HD
        self.heads_local = heads_local
        self.ffl = ff_local
        self.cols = 4 * self.local + 2 * ff_local
        self.windows = (GRID // WIN) ** 2
        self.images = tokens // (GRID * GRID)
        self.block = self.windows * SLOT
        self.rows = self.images * self.block
        self.groups = self.T * self.local // LANES
        a, b, c = 3 * self.local, 4 * self.local, 4 * self.local + ff_local
        self.at = {"qkv": (0, a), "proj": (a, b), "fc1": (b, c), "fc2": (c, self.cols)}
        self.gather_chunks = [(0, a), (a, c), (c, self.cols)]
        self.scatter_chunks = {"qkv": (0, a), "proj": (a, b), "fc1": (b, c), "fc2": (c, self.cols)}


def halves(cut):
    lo, hi = cut
    step = (hi - lo) // 2 // LANES * LANES
    return ((lo, step), (lo + step, hi - lo - step))


def step_kernel(plan, *refs):
    (x_ref, cot_ref, shard_ref, vec_ref, tab_ref, par_ref, mask_ref, hot_ref,
     out_ref, gin_ref, grad_ref, tot_ref, spill_big, spill_small, spill_inv, spill_qkv,
     W, G1, vecs, tabs, big, low, inv, qkv, gl, mid, bias, dscore, dbias, small, part,
     R0, R1, R2, R3, SR,
     ag_send, ag_recv, rs_send, rs_recv, sm_send, sm_recv, sp_sem) = refs
    Z, T, width, local, ffl = plan.Z, plan.T, plan.width, plan.local, plan.ffl
    block, images, rows = plan.block, plan.images, plan.rows
    L = LAYERS
    dp, t = lax.axis_index("dp"), lax.axis_index("tensor")
    z, y, x = dp // 4, (dp // 2) % 2, dp % 2
    other = 1 - t
    MESH = pl.DeviceIdType.MESH
    to_z = [{"dp": dp + 4 * (mix(z, j) - z)} for j in range(1, Z)]
    to_y, to_x, to_t = {"dp": flip(dp, 2)}, {"dp": flip(dp, 1)}, {"tensor": other}
    pending = []

    def remote(src, dst, send, recv, device):
        return pltpu.make_async_remote_copy(
            src_ref=src, dst_ref=dst, send_sem=send, recv_sem=recv, device_id=device, device_id_type=MESH
        )

    barrier = pltpu.get_barrier_semaphore()
    for device in to_z + [to_y, to_x, to_t]:
        pl.semaphore_signal(barrier, inc=1, device_id=device, device_id_type=MESH)

    xb = [(l, c) for l in range(L) for c in range(len(plan.gather_chunks))]

    def ag_copies(l, c):
        found = []
        for h, (lo, n) in enumerate(halves(plan.gather_chunks[c])):
            k = (l * len(plan.gather_chunks) + c) * 2 + h
            cs = pl.ds(lo, n)
            own = W.at[l, t, z, y, x, :, cs]
            plane = W.at[l, t, :, y, x, :, cs]
            if h == 0:
                wide, new2, new3 = W.at[l, t, :, :, x, :, cs], W.at[l, t, :, 1 - y, x, :, cs], W.at[l, t, :, :, 1 - x, :, cs]
                first, second = to_y, to_x
            else:
                wide, new2, new3 = W.at[l, t, :, y, :, :, cs], W.at[l, t, :, y, 1 - x, :, cs], W.at[l, t, :, 1 - y, :, :, cs]
                first, second = to_x, to_y
            s = lambda i, k=k: (ag_send.at[k, i], ag_recv.at[k, i])
            found.append(dict(
                p1=[remote(shard_ref.at[l, :, cs], own, *s(j), to_z[j]) for j in range(Z - 1)],
                p2=[remote(plane, plane, *s(Z - 1), first)],
                p3=[remote(wide, wide, *s(Z), second)],
                f1=[remote(plane, plane, *s(Z + 1), to_t)],
                f2=[remote(new2, new2, *s(Z + 2), to_t)],
                f3=[remote(new3, new3, *s(Z + 3), to_t)],
            ))
        return found

    def begin(copies):
        for copy in copies:
            copy.start()

    def arrive(copies):
        for copy in copies:
            copy.wait_recv()

    gathers = {key: ag_copies(*key) for key in xb}

    def ag(key, stage):
        for half in gathers[key]:
            if stage == 1:
                begin(half["p1"])
            elif stage == 2:
                arrive(half["p1"])
                begin(half["p2"] + half["f1"])
            elif stage == 3:
                arrive(half["p2"])
                begin(half["p3"] + half["f2"])
            elif stage == 4:
                arrive(half["p3"])
                begin(half["f3"])
            else:
                arrive(half["f1"] + half["f2"] + half["f3"])

    names = ("fc2", "fc1", "proj", "qkv")

    def grads_of(l):
        return G1 if l == L - 1 else W.at[L - 1]

    def rs_copies(l, name):
        found = []
        G = grads_of(l)
        for h, (lo, n) in enumerate(halves(plan.scatter_chunks[name])):
            k = (l * len(names) + names.index(name)) * 2 + h
            cs = pl.ds(lo, n)
            s = lambda i, k=k: (rs_send.at[k, i], rs_recv.at[k, i])
            if h == 0:
                away1, away2, first, second = G.at[t, :, :, 1 - x, :, cs], G.at[t, :, 1 - y, x, :, cs], to_x, to_y
            else:
                away1, away2, first, second = G.at[t, :, 1 - y, :, :, cs], G.at[t, :, y, 1 - x, :, cs], to_y, to_x
            found.append((cs, h, [
                [remote(G.at[other, :, :, :, :, cs], R0.at[l, :, :, :, :, cs], *s(0), to_t)],
                [remote(away1, R1.at[l, :, :, :, cs], *s(1), first)],
                [remote(away2, R2.at[l, :, :, cs], *s(2), second)],
                [remote(G.at[t, mix(z, j), y, x, :, cs], R3.at[l, j - 1, :, cs], *s(2 + j), to_z[j - 1]) for j in range(1, Z)],
            ]))
        return found

    scatters = {(l, name): rs_copies(l, name) for l in range(L) for name in names}

    def plus(a, b):
        return (a.astype(F32) + b.astype(F32)).astype(BF16)

    def rs(key, stage):
        l = key[0]
        G = grads_of(l)
        for cs, h, copies in scatters[key]:
            if stage > 0:
                arrive(copies[stage - 1])
            if stage == 1:
                @pl.loop(0, Z)
                def _(i):
                    G[t, i, :, :, :, cs] = plus(G[t, i, :, :, :, cs], R0[l, i, :, :, :, cs])
            elif stage == 2:
                @pl.loop(0, Z)
                def _(i):
                    for m in range(2):
                        where = (t, i, m, x) if h == 0 else (t, i, y, m)
                        G[(*where, slice(None), cs)] = plus(G[(*where, slice(None), cs)], R1[l, i, m, :, cs])
            elif stage == 3:
                @pl.loop(0, Z)
                def _(i):
                    G[t, i, y, x, :, cs] = plus(G[t, i, y, x, :, cs], R2[l, i, :, cs])
            elif stage == 4:
                total = G[t, z, y, x, :, cs].astype(F32)
                for j in range(1, Z):
                    total = total + R3[l, j - 1, :, cs].astype(F32)
                grad_ref[l, :, cs] = total
            if stage < 4:
                begin(copies[stage])

    def sm_copies():
        s = lambda i: (sm_send.at[i], sm_recv.at[i])
        found = [[remote(part.at[0], SR.at[0], *s(0), to_t)]]
        found.append([remote(part.at[1], SR.at[1], *s(1), to_x)])
        found.append([remote(part.at[2], SR.at[2], *s(2), to_y)])
        found.append([remote(part.at[3], SR.at[2 + j], *s(2 + j), to_z[j - 1]) for j in range(1, Z)])
        return found

    sums = sm_copies()

    def sm(stage):
        if stage > 0:
            arrive(sums[stage - 1])
        if stage == 0:
            part[0] = small[...]
        elif stage < 4:
            part[stage] = part[stage - 1] + SR[stage - 1]
        else:
            level = [part[3]] + [SR[2 + j] for j in range(1, Z)]
            while len(level) > 1:
                level = [level[i] + level[i + 1] for i in range(0, len(level), 2)]
            tot_ref[...] = level[0]
        if stage < 4:
            begin(sums[stage])

    queue = []

    def tick(n=1):
        for _ in range(min(n, len(queue))):
            queue.pop(0)()

    def drain_to(mark):
        while any(getattr(item, "mark", None) == mark for item in queue):
            queue.pop(0)()

    def push(fn, *args, mark=None):
        item = functools.partial(fn, *args)
        item.mark = mark
        queue.append(item)

    def spread(i, count, each=1):
        for k in range(count):
            taken = [queue.pop(0) for _ in range(min(each, len(queue)))]
            if taken:
                @pl.when(i == k)
                def _(taken=taken):
                    for item in taken:
                        item()

    def weight(l, tt, name, lo=None, n=None):
        a, b = plan.at[name]
        value = W[l, tt, :, :, :, :, a:b]
        return value.reshape(width, b - a)

    def put_grad(l, tt, name, first, value):
        a, b = plan.at[name]
        zs = value.shape[0] // (4 * plan.shard)
        grads_of(l)[tt, pl.ds(first, zs), :, :, :, a:b] = value.astype(BF16).reshape(zs, 2, 2, plan.shard, b - a)

    def row_slice(i):
        return pl.ds(pl.multiple_of(i * block, block), block)

    def param(l, name):
        return par_ref[l, PARAMS.index(name)][None, :]

    def add_small(l, row, value, lanes=slice(0, width)):
        small[l, row : row + 1, lanes] += jnp.sum(value, 0, keepdims=True)

    def permute(target, source, shift):
        runs = shift_segments(shift)

        @pl.loop(0, images)
        def _(i):
            base = pl.multiple_of(i * block, block)
            target[pl.ds(base, block), :] = jnp.zeros((block, width), F32)
            src, dst = source.at[pl.ds(base, block)], target.at[pl.ds(base, block)]
            for to, frm, n in runs:
                dst[to : to + n, :] = src[frm : frm + n, :]

    X1, AIN, MIX, X2, FIN = range(5)
    HID, SLOPE = 0, 1
    per = local // LANES

    def group_at(g, part_index):
        return (g // per) * 3 * local + part_index * local + (g % per) * LANES

    scale = HD ** (-0.5)
    low_masks, full_masks = head_masks(BF16), head_masks(F32)

    def win_rows(w):
        return pl.ds(pl.multiple_of(w * SLOT, SLOT), SLOT)

    def load_group(w, g):
        r = win_rows(w)
        return [qkv[r, group_at(g, n) : group_at(g, n) + LANES] for n in range(3)]

    def bias_of(l, w, g):
        per_group = LANES // HD
        mask = mask_ref[l % 2, lax.rem(w, plan.windows)]
        return jnp.concatenate([bias[l, g * per_group + h] + mask for h in range(per_group)], axis=0)

    def forward(l, r):
        @pl.loop(0, images)
        def _(i):
            rs_ = row_slice(i)
            normed, inverse = normalize(r[rs_, :])
            low[X1, rs_, :] = normed.astype(BF16)
            inv[0, rs_, :] = inverse
            low[AIN, rs_, :] = (normed * param(l, "n1g") + param(l, "n1b")).astype(BF16)

        if l == 0:
            drain_to((0, 0))
            prepare()
        else:
            drain_to((l, 0))

        @pl.loop(0, images)
        def _(i):
            rs_ = row_slice(i)
            a = low[AIN, rs_, :]
            for tt in range(T):
                value = dot(a, weight(l, tt, "qkv"))
                at = tt * 3 * local
                qb = vecs[tt, l, 1:2, 0:local]
                vb = vecs[tt, l, 2:3, 0:local]
                qkv[rs_, at : at + local] = ((value[:, :local] + qb) * scale).astype(BF16)
                qkv[rs_, at + local : at + 2 * local] = value[:, local : 2 * local].astype(BF16)
                qkv[rs_, at + 2 * local : at + 3 * local] = (value[:, 2 * local :] + vb).astype(BF16)
            spread(i, images)

        @pl.loop(0, images * plan.windows)
        def _(w):
            for g in range(plan.groups):
                q, k, v = load_group(w, g)
                attention = probabilities(stack_heads(q, low_masks), k, bias_of(l, w, g))
                mixed = dot(attention.astype(BF16), v)
                low[MIX, win_rows(w), g * LANES : (g + 1) * LANES] = merge_heads(mixed, full_masks).astype(BF16)
            spread(w, images * plan.windows)

        drain_to((l, 1))

        @pl.loop(0, images)
        def _(i):
            rs_ = row_slice(i)
            total = r[rs_, :] + param(l, "pb")
            for tt in range(T):
                total = total + dot(low[MIX, rs_, tt * local : (tt + 1) * local], weight(l, tt, "proj"), 1, 1)
            r[rs_, :] = total
            normed, inverse = normalize(total)
            low[X2, rs_, :] = normed.astype(BF16)
            inv[1, rs_, :] = inverse
            low[FIN, rs_, :] = (normed * param(l, "n2g") + param(l, "n2b")).astype(BF16)

        for tt in range(T):
            @pl.loop(0, images)
            def _(i, tt=tt):
                rs_ = row_slice(i)
                pre = dot(low[FIN, rs_, :], weight(l, tt, "fc1")) + vecs[tt, l, 0:1, :]
                activated, slope = gelu_parts(pre)
                big[HID, rs_, tt * ffl : (tt + 1) * ffl] = activated.astype(BF16)
                big[SLOPE, rs_, tt * ffl : (tt + 1) * ffl] = slope.astype(BF16)
                spread(i, images)

        drain_to((l, 2))

        @pl.loop(0, images)
        def _(i):
            rs_ = row_slice(i)
            total = r[rs_, :] + param(l, "f2b")
            for tt in range(T):
                total = total + dot(big[HID, rs_, tt * ffl : (tt + 1) * ffl], weight(l, tt, "fc2"), 1, 1)
            r[rs_, :] = total
            spread(i, images)

    def prepare():
        bias[...] = jnp.zeros_like(bias)
        for tt in range(T):
            @pl.when(t == tt)
            def _(tt=tt):
                vecs[tt] = vec_ref[...]
                tabs[tt] = tab_ref[...]
        arrive(small_in)

        for l in range(L):
            table = jnp.concatenate([tabs[tt, l] for tt in range(T)], axis=0).astype(BF16)

            @pl.loop(0, WIN * WIN)
            def _(i, table=table, l=l):
                line = dot(table, hot_ref[i], 1, 1)
                bias[l, :, pl.ds(i, 1), :] = line[:, None, :]

    def backward(l, g):
        @pl.loop(0, images)
        def _(i):
            rs_ = row_slice(i)
            value = g[rs_, :]
            add_small(l, 5, value)
            gl[rs_, :] = value.astype(BF16)

        half = width // 2
        for tt in range(T):
            fcols = slice(tt * ffl, (tt + 1) * ffl)

            @pl.loop(0, images)
            def _(i, tt=tt, fcols=fcols):
                rs_ = row_slice(i)
                dpre = dot(gl[rs_, :], weight(l, tt, "fc2")) * big[SLOPE, rs_, fcols].astype(F32)
                sums_ = jnp.sum(dpre, 0, keepdims=True)
                for m in range(ffl // width):
                    small[l, 8 + tt * (ffl // width) + m : 9 + tt * (ffl // width) + m, :] += sums_[:, m * width : (m + 1) * width]
                big[SLOPE, rs_, fcols] = dpre.astype(BF16)
                spread(i, images)

            @pl.loop(0, 2)
            def _(m, tt=tt, fcols=fcols):
                lanes = pl.ds(pl.multiple_of(m * half, half), half)
                put_grad(l, tt, "fc2", m * (Z // 2), dot(gl[:, lanes], big[HID, :, fcols], 0, 0))
                spread(m, 2)

        rs((l, "fc2"), 0)
        for tt in range(T):
            fcols = slice(tt * ffl, (tt + 1) * ffl)

            @pl.loop(0, 2)
            def _(m, tt=tt, fcols=fcols):
                lanes = pl.ds(pl.multiple_of(m * half, half), half)
                put_grad(l, tt, "fc1", m * (Z // 2), dot(low[FIN, :, lanes], big[SLOPE, :, fcols], 0, 0))
                spread(m, 2)

        rs((l, "fc1"), 0)
        for stage in range(1, 5):
            push(rs, (l, "fc2"), stage)
            push(rs, (l, "fc1"), stage)

        @pl.loop(0, images)
        def _(i):
            rs_ = row_slice(i)
            dffn = dot(big[SLOPE, rs_, 0:ffl], weight(l, 0, "fc1"), 1, 1)
            for tt in range(1, T):
                dffn = dffn + dot(big[SLOPE, rs_, tt * ffl : (tt + 1) * ffl], weight(l, tt, "fc1"), 1, 1)
            normed = low[X2, rs_, :].astype(F32)
            add_small(l, 3, dffn * normed)
            add_small(l, 4, dffn)
            g_mid = g[rs_, :] + norm_back(dffn, normed, inv[1, rs_, :], param(l, "n2g"))
            add_small(l, 2, g_mid)
            g[rs_, :] = g_mid
            gl[rs_, :] = g_mid.astype(BF16)
            spread(i, images)

        if l > 0:
            fetch("big")
        for tt in range(T):
            @pl.loop(0, 2)
            def _(m, tt=tt):
                lanes = pl.ds(pl.multiple_of(m * half, half), half)
                put_grad(l, tt, "proj", m * (Z // 2), dot(gl[:, lanes], low[MIX, :, tt * local : (tt + 1) * local], 0, 0))
        rs((l, "proj"), 0)
        for stage in range(1, 5):
            push(rs, (l, "proj"), stage)

        @pl.loop(0, images)
        def _(i):
            rs_ = row_slice(i)
            for tt in range(T):
                low[MIX, rs_, tt * local : (tt + 1) * local] = dot(gl[rs_, :], weight(l, tt, "proj")).astype(BF16)

        dscore[...] = jnp.zeros_like(dscore)
        dbias[...] = jnp.zeros_like(dbias)

        @pl.loop(0, images * plan.windows)
        def _(w):
            r = win_rows(w)
            for gg in range(plan.groups):
                q, k, v = load_group(w, gg)
                dm = low[MIX, r, gg * LANES : (gg + 1) * LANES]
                q_stacked, dm_stacked = stack_heads(q, low_masks), stack_heads(dm, low_masks)
                attention = probabilities(q_stacked, k, bias_of(l, w, gg))
                dattention = dot(dm_stacked, v, 1, 1)
                inner = jnp.sum(attention * dattention, -1, keepdims=True)
                dscores = attention * (dattention - inner)
                dscore[pl.ds(gg * 4, 4)] += dscores.reshape(4, SLOT, SLOT)
                dl = dscores.astype(BF16)
                dq = merge_heads(dot(dl, k), full_masks) * scale
                dk = dot(dl, q_stacked, 0, 0)
                dv = dot(attention.astype(BF16), dm_stacked, 0, 0)
                for n, value in enumerate((dq, dk, dv)):
                    qkv[r, group_at(gg, n) : group_at(gg, n) + LANES] = value.astype(BF16)
                    if n != 1:
                        dbias[n // 2, :, gg * LANES : (gg + 1) * LANES] += jnp.sum(value.reshape(SLOT // 8, 8, LANES), 0)
            spread(w, images * plan.windows)

        add_small(l, 6, dbias[0])
        add_small(l, 7, dbias[1])
        if l > 0:
            fetch("mix")
        for tt in range(T):
            at = tt * 3 * local

            @pl.loop(0, 2)
            def _(m, tt=tt, at=at):
                lanes = pl.ds(pl.multiple_of(m * half, half), half)
                put_grad(l, tt, "qkv", m * (Z // 2), dot(low[AIN, :, lanes], qkv[:, at : at + 3 * local], 0, 0))
        rs((l, "qkv"), 0)
        for stage in range(1, 5):
            push(rs, (l, "qkv"), stage)

        @pl.loop(0, images)
        def _(i):
            rs_ = row_slice(i)
            dattn = dot(qkv[rs_, 0 : 3 * local], weight(l, 0, "qkv"), 1, 1)
            for tt in range(1, T):
                dattn = dattn + dot(qkv[rs_, tt * 3 * local : (tt + 1) * 3 * local], weight(l, tt, "qkv"), 1, 1)
            normed = low[X1, rs_, :].astype(F32)
            add_small(l, 0, dattn * normed)
            add_small(l, 1, dattn)
            g[rs_, :] = g[rs_, :] + norm_back(dattn, normed, inv[0, rs_, :], param(l, "n1g"))
            spread(i, images)

        if l > 0:
            fetch("rest")

        n_heads = T * plan.heads_local
        accumulated = jnp.zeros((n_heads, TABLE_LANES), F32)

        def table_step(i, acc):
            line = dscore[:, pl.ds(i, 1), :].reshape(n_heads, SLOT)
            high = line.astype(BF16)
            rest = line - high.astype(F32)
            middle = rest.astype(BF16)
            least = (rest - middle.astype(F32)).astype(BF16)
            three = jnp.concatenate([high, middle, least], axis=0)
            out = dot(three, hot_ref[i])
            return acc + ((out[2 * n_heads :] + out[n_heads : 2 * n_heads]) + out[:n_heads])

        accumulated = lax.fori_loop(0, WIN * WIN, table_step, accumulated)
        hl = n_heads // 2
        small[l, 16 : 16 + hl, 0:TABLE_LANES] = accumulated[:hl]
        small[l, 16 : 16 + hl, TABLE_LANES : 2 * TABLE_LANES] = accumulated[hl:]

    lows = [(low.at[n], spill_small.at[n]) for n in range(5)]
    moves = {
        "ain": [lows[X1], lows[AIN]], "mix": [lows[MIX], lows[X2], lows[FIN]],
        "inv": [(inv, spill_inv)], "qkv": [(qkv, spill_qkv)], "big": [(big, spill_big)],
    }
    order = [pair for name in ("ain", "mix", "inv", "qkv", "big") for pair in moves[name]]
    fetched = []

    def spill():
        copies = [pltpu.make_async_copy(a, b, sp_sem.at[n]) for n, (a, b) in enumerate(order)]
        begin(copies)
        for copy in copies:
            copy.wait()

    def fetch(name):
        which = {
            "big": [7, 3, 4], "mix": [2], "rest": [0, 1, 5, 6],
        }[name]
        for n in which:
            a, b = order[n]
            copy = pltpu.make_async_copy(b, a, sp_sem.at[n])
            copy.start()
            fetched.append(copy)

    def sent(found):
        for copies in found:
            for half in copies:
                for group in half.values():
                    for copy in group:
                        copy.wait_send()

    small_in = [
        remote(vec_ref, vecs.at[t], sm_send.at[2 + Z], sm_recv.at[2 + Z], to_t),
        remote(tab_ref, tabs.at[t], sm_send.at[3 + Z], sm_recv.at[3 + Z], to_t),
    ]
    pl.semaphore_wait(barrier, Z - 1 + 3)
    ag((0, 0), 1)
    begin(small_in)
    for c in range(1, len(plan.gather_chunks)):
        ag((0, c), 1)
    for l in range(L):
        W[l, t, z, y, x] = shard_ref[l]
    small[...] = jnp.zeros_like(small)

    for stage in (2, 3, 4):
        push(ag, (0, 0), stage)
    push(ag, (0, 0), 5, mark=(0, 0))
    push(ag, (0, 1), 2)
    push(ag, (0, 2), 2)
    push(ag, (0, 1), 3)
    for c in range(3):
        push(ag, (1, c), 1)
    push(ag, (0, 2), 3)
    push(ag, (0, 1), 4)
    push(ag, (0, 2), 4)
    push(ag, (0, 1), 5, mark=(0, 1))
    push(ag, (1, 0), 2)
    push(ag, (1, 1), 2)
    push(ag, (0, 2), 5, mark=(0, 2))
    push(ag, (1, 0), 3)
    push(ag, (1, 2), 2)
    push(ag, (1, 1), 3)
    push(ag, (1, 0), 4)
    push(ag, (1, 2), 3)
    push(ag, (1, 1), 4)
    push(ag, (1, 0), 5, mark=(1, 0))
    push(ag, (1, 2), 4)
    push(ag, (1, 1), 5, mark=(1, 1))
    push(ag, (1, 2), 5, mark=(1, 2))

    @pl.loop(0, images)
    def _(i):
        rs_ = row_slice(i)
        out_ref[rs_, :] = x_ref[rs_, :].astype(F32)

    forward(0, out_ref)
    spill()
    permute(mid, out_ref, SHIFT)
    forward(1, mid)
    permute(out_ref, mid, GRID - SHIFT)

    @pl.loop(0, images)
    def _(i):
        rs_ = row_slice(i)
        gin_ref[rs_, :] = cot_ref[rs_, :].astype(F32)

    permute(mid, gin_ref, SHIFT)
    backward(1, mid)
    permute(gin_ref, mid, GRID - SHIFT)
    for copy in fetched:
        copy.wait()
    sent(gathers.values())
    backward(0, gin_ref)
    sm(0)
    tick(1)
    sm(1)
    tick(1)
    sm(2)
    tick(1)
    sm(3)
    tick(1)
    sm(4)
    tick(len(queue))
    for found in scatters.values():
        for _, _, groups in found:
            for group in groups:
                for copy in group:
                    copy.wait_send()
    for group in sums + [small_in]:
        for copy in group:
            copy.wait_send()


def fast_device(
    inputs, cotangent, region_ids, rel_index, norm1_gain, norm1_bias, w_qkv, qv_bias, bias_table, w_proj,
    proj_bias, norm2_gain, norm2_bias, w_fc1, fc1_bias, w_fc2, fc2_bias,
):
    t_index = lax.axis_index("tensor")
    tokens, width = inputs.shape
    plan = Plan(lax.axis_size("dp"), tokens, width, fc1_bias.shape[1], bias_table.shape[1])
    win_tokens = WIN * WIN
    pad = SLOT - win_tokens
    L, T, Z, local, ffl, hl = LAYERS, plan.T, plan.Z, plan.local, plan.ffl, plan.heads_local
    R, C, M = plan.shard, plan.cols, plan.rows

    def padded(array):
        spread_ = array.reshape(tokens // win_tokens, win_tokens, width)
        return jnp.pad(spread_, ((0, 0), (0, pad), (0, 0))).reshape(M, width)

    shards = jnp.stack([pack_weights(w_qkv[l], w_proj[l], w_fc1[l], w_fc2[l]) for l in range(L)])
    vec = jnp.zeros((L, 8, ffl), F32)
    vec = vec.at[:, 0].set(fc1_bias.astype(F32))
    vec = vec.at[:, 1:3, :local].set(qv_bias.astype(F32))
    tab = jnp.pad(bias_table.astype(F32), ((0, 0), (0, 0), (0, TABLE_LANES - TABLE)))
    params = jnp.stack([norm1_gain, norm1_bias, proj_bias, norm2_gain, norm2_bias, fc2_bias], axis=1).astype(F32)
    params = jnp.pad(params, ((0, 0), (0, 2), (0, 0)))
    index_padded = jnp.pad(rel_index, ((0, pad), (0, pad)), constant_values=-1)
    hot = (index_padded[:, :, None] == jnp.arange(TABLE_LANES, dtype=jnp.int32)).astype(BF16)
    regions = region_ids.reshape(plan.windows, win_tokens)
    shift_mask = jnp.where(regions[:, :, None] == regions[:, None, :], 0.0, MASKED).astype(F32)
    mask = jnp.stack([jnp.zeros_like(shift_mask), shift_mask])
    mask = jnp.pad(mask, ((0, 0), (0, 0), (0, pad), (0, 0)))
    mask = jnp.pad(mask, ((0, 0), (0, 0), (0, 0), (0, pad)), constant_values=PADDED)

    vmem = pl.BlockSpec(memory_space=pltpu.VMEM)
    anywhere = pl.BlockSpec(memory_space=pl.ANY)
    n_ag, n_rs = L * 3 * 2, L * 4 * 2
    DMA = pltpu.SemaphoreType.DMA
    outs = pl.pallas_call(
        functools.partial(step_kernel, plan),
        out_shape=(
            jax.ShapeDtypeStruct((M, width), F32),
            jax.ShapeDtypeStruct((M, width), F32),
            jax.ShapeDtypeStruct((L, R, C), F32),
            jax.ShapeDtypeStruct((L, SMALL_ROWS, width), F32),
            jax.ShapeDtypeStruct((2, M, T * ffl), BF16),
            jax.ShapeDtypeStruct((5, M, width), BF16),
            jax.ShapeDtypeStruct((2, M, 1), F32),
            jax.ShapeDtypeStruct((M, 3 * width), BF16),
        ),
        in_specs=[vmem] * 8,
        out_specs=(vmem,) * 4 + (anywhere,) * 4,
        scratch_shapes=[
            pltpu.VMEM((L, T, Z, 2, 2, R, C), BF16),
            pltpu.VMEM((T, Z, 2, 2, R, C), BF16),
            pltpu.VMEM((T, L, 8, ffl), F32),
            pltpu.VMEM((T, L, hl, TABLE_LANES), F32),
            pltpu.VMEM((2, M, T * ffl), BF16),
            pltpu.VMEM((5, M, width), BF16),
            pltpu.VMEM((2, M, 1), F32),
            pltpu.VMEM((M, 3 * width), BF16),
            pltpu.VMEM((M, width), BF16),
            pltpu.VMEM((M, width), F32),
            pltpu.VMEM((L, T * hl, SLOT, SLOT), F32),
            pltpu.VMEM((T * hl, SLOT, SLOT), F32),
            pltpu.VMEM((2, 8, width), F32),
            pltpu.VMEM((L, SMALL_ROWS, width), F32),
            pltpu.VMEM((4, L, SMALL_ROWS, width), F32),
            pltpu.VMEM((L, Z, 2, 2, R, C), BF16),
            pltpu.VMEM((L, Z, 2, R, C), BF16),
            pltpu.VMEM((L, Z, R, C), BF16),
            pltpu.VMEM((L, Z - 1, R, C), BF16),
            pltpu.VMEM((Z + 2, L, SMALL_ROWS, width), F32),
            DMA((n_ag, Z + 4)),
            DMA((n_ag, Z + 4)),
            DMA((n_rs, Z + 2)),
            DMA((n_rs, Z + 2)),
            DMA((Z + 4,)),
            DMA((Z + 4,)),
            DMA((8,)),
        ],
        compiler_params=pltpu.CompilerParams(
            collective_id=0, has_side_effects=True, vmem_limit_bytes=67043328
        ),
        name="whole_step",
    )(padded(inputs), padded(cotangent), shards, vec, tab, params, mask, hot)
    out, g_in, grads, total = outs[:4]

    def unpadded(array):
        return array.reshape(-1, SLOT, width)[:, :win_tokens].reshape(tokens, width)

    qv_total = lax.dynamic_slice_in_dim(total[:, 6:8], t_index * local, local, 2)
    fc1_total = total[:, 8 : 8 + T * ffl // width].reshape(L, T * ffl)
    fc1_total = lax.dynamic_slice_in_dim(fc1_total, t_index * ffl, ffl, 1)
    table_total = lax.dynamic_slice_in_dim(total[:, 16 : 16 + hl], t_index * TABLE_LANES, TABLE_LANES, 2)[..., :TABLE]
    a, b, c = 3 * local, 4 * local, 4 * local + ffl
    return (
        unpadded(out), unpadded(g_in), total[:, 0], total[:, 1],
        grads[..., :a].reshape(L, R, 3, local).transpose(0, 2, 1, 3),
        qv_total, table_total,
        grads[..., a:b].transpose(0, 2, 1),
        total[:, 2], total[:, 3], total[:, 4],
        grads[..., b:c], fc1_total,
        grads[..., c:].transpose(0, 2, 1),
        total[:, 5],
    )


def one_kernel_fits(inputs, bias_table, fc1_bias):
    n_dp, n_t = lax.axis_size("dp"), lax.axis_size("tensor")
    tokens, width = inputs.shape
    z = n_dp // 4
    heads_local = bias_table.shape[1]
    return (
        n_t == 2 and n_dp % 4 == 0 and z >= 2 and z & (z - 1) == 0
        and heads_local * HD % LANES == 0 and heads_local % 8 == 0 and heads_local <= 8
        and width // n_dp % 16 == 0 and width == 2 * TABLE_LANES and fc1_bias.shape[1] % width == 0
        and 8 + 2 * fc1_bias.shape[1] // width <= 16
        and tokens % (GRID * GRID) == 0 and tokens <= 4 * GRID * GRID
    )


def choose(*args):
    if one_kernel_fits(args[0], args[8], args[14]):
        return fast_device(*args)
    return per_device(*args)


def solution(mesh):
    in_specs = (
        P(("dp", "tensor"), None),
        P(("dp", "tensor"), None),
        P(),
        P(),
        P(),
        P(),
        P(None, None, "dp", "tensor"),
        P(None, None, "tensor"),
        P(None, "tensor", None),
        P(None, "tensor", "dp"),
        P(),
        P(),
        P(),
        P(None, "dp", "tensor"),
        P(None, "tensor"),
        P(None, "tensor", "dp"),
        P(),
    )
    out_specs = (
        P(("dp", "tensor"), None),
        P(("dp", "tensor"), None),
        P(),
        P(),
        P(None, None, "dp", "tensor"),
        P(None, None, "tensor"),
        P(None, "tensor", None),
        P(None, "tensor", "dp"),
        P(),
        P(),
        P(),
        P(None, "dp", "tensor"),
        P(None, "tensor"),
        P(None, "tensor", "dp"),
        P(),
    )
    return jax.shard_map(
        choose, mesh=mesh, in_specs=in_specs, out_specs=out_specs, check_vma=False
    )
```

profile of v0, /device:TPU:0, one launch (start us, length us, event | category | flops | bytes accessed | tf_op | source)
XLA Modules:
  0.0 381.6 jit_solution(12610289038022874143)
XLA Ops:
  0.7 0.8 slice_bitcast_fusion.7
  1.5 0.9 slice_bitcast_fusion.5
  2.4 1.0 slice_bitcast_fusion.4
  3.4 0.7 slice_bitcast_fusion.10
  4.1 0.9 pad_maximum_fusion.refs_2_
  5.0 1.7 fusion.refs_7_
  7.0 1.1 pad.40
  8.4 1.1 pad.41
  9.7 0.7 pad_select_fusion.refs_6_
  11.1 1.5 scatter.14.refs_3_
  14.0 347.5 %whole_step.1 = (f32[1024,512]{1,0:T(8,128)}, f32[1024,512]{1,0:T(8,128)}, f32[2,32,3072]{2,1,0:T(8,128)}, f32[2,24,512]{2,1,0:T(8,128)}, bf16[2,1024,2048]{2,1,...) custom-call(bf16[1024,512]{1,0:T(8,128)(2,1)} %bitcast.73, ...), custom_call_target="tpu_custom_call" | custom-call | tf_op jit(solution)/shard_map/whole_step/pallas_call | solution.py:1159
  361.5 0.8 slice.133
  362.2 0.7 constant_dynamic-slice_fusion.1
  362.9 0.8 slice.132
  364.3 0.8 slice_bitcast_fusion.8
  365.7 1.1 fusion.1
  370.3 1.9 slice_bitcast_fusion
  372.2 0.9 slice.131
  373.3 0.7 copy.44
  374.0 1.5 slice_bitcast_fusion.1
  375.4 1.7 slice.143
  377.1 1.4 reshape.155
  378.5 1.7 slice.144
  380.2 1.4 reshape.157
  (56 shorter events, 7.6 us)
Async XLA Ops:
  0.6 4.4 %copy-start.2 = (s32[49,49]{1,0:T(8,128)S(1)}, s32[49,49]{1,0:T(8,128)}, u32[]{:S(2)}) copy-start(s32[49,49]{1,0:T(8,128)} %param.24) | copy-start | bytes 28816
  2.4 4.3 %copy-start = (bf16[784,512]{1,0:T(8,128)(2,1)S(1)}, bf16[784,512]{1,0:T(8,128)(2,1)}, u32[]{:S(2)}) copy-start(bf16[784,512]{1,0:T(8,128)(2,1)} %param.21) | copy-start | bytes 2408452
  6.7 1.4 copy-start.1
  8.0 1.4 copy-start.12
  8.1 2.4 copy-start.4
  8.1 3.0 copy-start.5
  8.1 4.5 %copy-start.6 = (bf16[2,512]{1,0:T(2,128)(2,1)S(1)}, bf16[2,512]{1,0:T(2,128)(2,1)}, u32[]{:S(2)}) copy-start(bf16[2,512]{1,0:T(2,128)(2,1)} %param.25) | copy-start | bytes 6148
  8.1 4.5 %copy-start.7 = (bf16[2,512]{1,0:T(2,128)(2,1)S(1)}, bf16[2,512]{1,0:T(2,128)(2,1)}, u32[]{:S(2)}) copy-start(bf16[2,512]{1,0:T(2,128)(2,1)} %param.26) | copy-start | bytes 6148
  8.1 4.5 %copy-start.8 = (bf16[2,512]{1,0:T(2,128)(2,1)S(1)}, bf16[2,512]{1,0:T(2,128)(2,1)}, u32[]{:S(2)}) copy-start(bf16[2,512]{1,0:T(2,128)(2,1)} %param.31) | copy-start | bytes 6148
  8.1 4.5 %copy-start.9 = (bf16[2,512]{1,0:T(2,128)(2,1)S(1)}, bf16[2,512]{1,0:T(2,128)(2,1)}, u32[]{:S(2)}) copy-start(bf16[2,512]{1,0:T(2,128)(2,1)} %param.32) | copy-start | bytes 6148
  8.1 4.5 %copy-start.10 = (bf16[2,512]{1,0:T(2,128)(2,1)S(1)}, bf16[2,512]{1,0:T(2,128)(2,1)}, u32[]{:S(2)}) copy-start(bf16[2,512]{1,0:T(2,128)(2,1)} %param.33) | copy-start | bytes 6148
  8.1 4.5 %copy-start.11 = (bf16[2,512]{1,0:T(2,128)(2,1)S(1)}, bf16[2,512]{1,0:T(2,128)(2,1)}, u32[]{:S(2)}) copy-start(bf16[2,512]{1,0:T(2,128)(2,1)} %param.37) | copy-start | bytes 6148
  8.1 5.2 %copy-start.3 = (bf16[2,8,169]{2,1,0:T(8,128)(2,1)S(1)}, bf16[2,8,169]{2,1,0:T(8,128)(2,1)}, u32[]{:S(2)}) copy-start(bf16[2,8,169]{2,1,0:T(8,128)(2,1)} %param.29) | copy-start | bytes 16228
where the time goes:
time: 382 us
  Pallas kernels  348 us (91%)
  local copies, waits for them, and re-layouts  27.9 us (7%)
  other arithmetic  5.27 us (1%)
    pallas_call x1, Pallas kernels, fast_device(): pl.pallas_call(functools.partial(step_kernel, plan), out_shape=(jax.Shape...  348 us

commit v1 on v0

--- a/solution.py
+++ b/solution.py
@@ -472,6 +472,7 @@
 
 SMALL_ROWS = 24
 TABLE_LANES = 256
+PACK = LANES // HD
 PARAMS = ("n1g", "n1b", "pb", "n2g", "n2b", "f2b")
 
 
@@ -697,21 +698,29 @@
     queue = []
 
     def tick(n=1):
-        for _ in range(min(n, len(queue))):
-            queue.pop(0)()
+        while n > 0 and queue:
+            item = queue.pop(0)
+            if item is not None:
+                item()
+                n -= 1
 
     def drain_to(mark):
         while any(getattr(item, "mark", None) == mark for item in queue):
-            queue.pop(0)()
+            item = queue.pop(0)
+            if item is not None:
+                item()
 
     def push(fn, *args, mark=None):
         item = functools.partial(fn, *args)
         item.mark = mark
         queue.append(item)
 
+    def gap(n=1):
+        queue.extend([None] * n)
+
     def spread(i, count, each=1):
         for k in range(count):
-            taken = [queue.pop(0) for _ in range(min(each, len(queue)))]
+            taken = [item for item in (queue.pop(0) for _ in range(min(each, len(queue)))) if item is not None]
             if taken:
                 @pl.when(i == k)
                 def _(taken=taken):
@@ -766,9 +775,20 @@
         return [qkv[r, group_at(g, n) : group_at(g, n) + LANES] for n in range(3)]
 
     def bias_of(l, w, g):
-        per_group = LANES // HD
-        mask = mask_ref[l % 2, lax.rem(w, plan.windows)]
-        return jnp.concatenate([bias[l, g * per_group + h] + mask for h in range(per_group)], axis=0)
+        if l % 2 == 0:
+            return bias[l * plan.groups + g]
+        return bias[(lax.rem(w, plan.windows) + 1) * plan.groups + g]
+
+    def column_softmax(scores):
+        exponent = jnp.exp(scores - jnp.max(scores, 0, keepdims=True))
+        return exponent * (1.0 / jnp.sum(exponent, 0, keepdims=True))
+
+    def pick_heads(stacked):
+        lane = lax.broadcasted_iota(jnp.int32, (SLOT, LANES), 1)
+        out = stacked[(PACK - 1) * SLOT :]
+        for h in range(PACK - 2, -1, -1):
+            out = jnp.where(lane < (h + 1) * HD, stacked[h * SLOT : (h + 1) * SLOT], out)
+        return out
 
     def forward(l, r):
         @pl.loop(0, images)
@@ -780,8 +800,8 @@
             low[AIN, rs_, :] = (normed * param(l, "n1g") + param(l, "n1b")).astype(BF16)
 
         if l == 0:
+            prepare()
             drain_to((0, 0))
-            prepare()
         else:
             drain_to((l, 0))
 
@@ -803,9 +823,9 @@
         def _(w):
             for g in range(plan.groups):
                 q, k, v = load_group(w, g)
-                attention = probabilities(stack_heads(q, low_masks), k, bias_of(l, w, g))
-                mixed = dot(attention.astype(BF16), v)
-                low[MIX, win_rows(w), g * LANES : (g + 1) * LANES] = merge_heads(mixed, full_masks).astype(BF16)
+                attention = column_softmax(dot(k, stack_heads(q, low_masks), 1, 1) + bias_of(l, w, g))
+                mixed = dot(attention.astype(BF16), v, 0, 0)
+                low[MIX, win_rows(w), g * LANES : (g + 1) * LANES] = pick_heads(mixed).astype(BF16)
             spread(w, images * plan.windows)
 
         drain_to((l, 1))
@@ -852,13 +872,27 @@
                 tabs[tt] = tab_ref[...]
         arrive(small_in)
 
-        for l in range(L):
-            table = jnp.concatenate([tabs[tt, l] for tt in range(T)], axis=0).astype(BF16)
-
-            @pl.loop(0, WIN * WIN)
-            def _(i, table=table, l=l):
-                line = dot(table, hot_ref[i], 1, 1)
-                bias[l, :, pl.ds(i, 1), :] = line[:, None, :]
+        heads = T * plan.heads_local
+        table = jnp.concatenate([tabs[tt, l] for l in range(L) for tt in range(T)], axis=0).astype(BF16)
+        shape = (L * heads, PACK * SLOT)
+        own = lax.broadcasted_iota(jnp.int32, shape, 0) % PACK == lax.broadcasted_iota(jnp.int32, shape, 1) // SLOT
+        shape = (L * plan.groups, L * heads)
+        gather = (lax.broadcasted_iota(jnp.int32, shape, 1) // PACK == lax.broadcasted_iota(jnp.int32, shape, 0)).astype(BF16)
+
+        @pl.loop(0, WIN)
+        def _(a):
+            for b in range(WIN):
+                j = a * WIN + b
+                line = dot(table, jnp.concatenate([hot_ref[j]] * PACK, axis=0), 1, 1)
+                line = dot(gather, jnp.where(own, line, 0.0).astype(BF16))
+                bias[0 : L * plan.groups, pl.ds(j, 1), :] = line[:, None, :]
+            spread(a, WIN)
+
+        for w in reversed(range(plan.windows)):
+            for g in range(plan.groups):
+                bias[(w + 1) * plan.groups + g] = bias[plan.groups + g] + mask_ref[w + 1]
+        for g in range(plan.groups):
+            bias[g] = bias[g] + mask_ref[0]
 
     def backward(l, g):
         @pl.loop(0, images)
@@ -899,9 +933,24 @@
                 spread(m, 2)
 
         rs((l, "fc1"), 0)
-        for stage in range(1, 5):
-            push(rs, (l, "fc2"), stage)
-            push(rs, (l, "fc1"), stage)
+        gap(1)
+        push(rs, (l, "fc2"), 1)
+        gap(1)
+        push(rs, (l, "fc1"), 1)
+        push(rs, (l, "fc2"), 2)
+        gap(3)
+        push(rs, (l, "fc1"), 2)
+        push(rs, (l, "fc2"), 3)
+        push(rs, (l, "proj"), 1)
+        gap(1)
+        push(rs, (l, "fc1"), 3)
+        push(rs, (l, "proj"), 2)
+        push(rs, (l, "fc2"), 4)
+        gap(1)
+        push(rs, (l, "proj"), 3)
+        push(rs, (l, "fc1"), 4)
+        push(rs, (l, "proj"), 4)
+        gap(2)
 
         @pl.loop(0, images)
         def _(i):
@@ -926,9 +975,6 @@
                 lanes = pl.ds(pl.multiple_of(m * half, half), half)
                 put_grad(l, tt, "proj", m * (Z // 2), dot(gl[:, lanes], low[MIX, :, tt * local : (tt + 1) * local], 0, 0))
         rs((l, "proj"), 0)
-        for stage in range(1, 5):
-            push(rs, (l, "proj"), stage)
-
         @pl.loop(0, images)
         def _(i):
             rs_ = row_slice(i)
@@ -945,15 +991,15 @@
                 q, k, v = load_group(w, gg)
                 dm = low[MIX, r, gg * LANES : (gg + 1) * LANES]
                 q_stacked, dm_stacked = stack_heads(q, low_masks), stack_heads(dm, low_masks)
-                attention = probabilities(q_stacked, k, bias_of(l, w, gg))
-                dattention = dot(dm_stacked, v, 1, 1)
-                inner = jnp.sum(attention * dattention, -1, keepdims=True)
+                attention = column_softmax(dot(k, q_stacked, 1, 1) + bias_of(l, w, gg))
+                dattention = dot(v, dm_stacked, 1, 1)
+                inner = jnp.sum(attention * dattention, 0, keepdims=True)
                 dscores = attention * (dattention - inner)
-                dscore[pl.ds(gg * 4, 4)] += dscores.reshape(4, SLOT, SLOT)
+                dscore[gg] += dscores
                 dl = dscores.astype(BF16)
-                dq = merge_heads(dot(dl, k), full_masks) * scale
-                dk = dot(dl, q_stacked, 0, 0)
-                dv = dot(attention.astype(BF16), dm_stacked, 0, 0)
+                dq = pick_heads(dot(dl, k, 0, 0)) * scale
+                dk = dot(dl, q_stacked)
+                dv = dot(attention.astype(BF16), dm_stacked)
                 for n, value in enumerate((dq, dk, dv)):
                     qkv[r, group_at(gg, n) : group_at(gg, n) + LANES] = value.astype(BF16)
                     if n != 1:
@@ -972,8 +1018,41 @@
                 lanes = pl.ds(pl.multiple_of(m * half, half), half)
                 put_grad(l, tt, "qkv", m * (Z // 2), dot(low[AIN, :, lanes], qkv[:, at : at + 3 * local], 0, 0))
         rs((l, "qkv"), 0)
-        for stage in range(1, 5):
-            push(rs, (l, "qkv"), stage)
+        gap(4)
+        push(rs, (l, "qkv"), 1)
+        gap(5)
+        push(rs, (l, "qkv"), 2)
+        if l > 0:
+            gap(4)
+        push(rs, (l, "qkv"), 3)
+        if l > 0:
+            gap(4)
+        push(rs, (l, "qkv"), 4)
+
+        spare = 8
+        shape = (PACK * spare, PACK * SLOT)
+        own = lax.broadcasted_iota(jnp.int32, shape, 0) // spare == lax.broadcasted_iota(jnp.int32, shape, 1) // SLOT
+
+        def table_step(a, acc):
+            for b in range(WIN):
+                j = a * WIN + b
+                line = dscore[:, pl.ds(j, 1), :].reshape(spare, PACK * SLOT)
+                line = jnp.where(own, jnp.concatenate([line] * PACK, axis=0), 0.0)
+                high = line.astype(BF16)
+                rest = line - high.astype(F32)
+                middle = rest.astype(BF16)
+                least = (rest - middle.astype(F32)).astype(BF16)
+                three = jnp.concatenate([high, middle, least], axis=0)
+                out = dot(three, jnp.concatenate([hot_ref[j]] * PACK, axis=0))
+                n = PACK * spare
+                acc = acc + ((out[2 * n :] + out[n : 2 * n]) + out[:n])
+            spread(a, WIN)
+            return acc
+
+        total = lax.fori_loop(0, WIN, table_step, jnp.zeros((PACK * spare, TABLE_LANES), F32))
+        for hh in range(PACK):
+            to, lanes = 16 + hh % 2 * plan.groups, slice(hh // 2 * TABLE_LANES, (hh // 2 + 1) * TABLE_LANES)
+            small[l, to : to + plan.groups, lanes] = total[hh * spare : hh * spare + plan.groups]
 
         @pl.loop(0, images)
         def _(i):
@@ -990,24 +1069,6 @@
         if l > 0:
             fetch("rest")
 
-        n_heads = T * plan.heads_local
-        accumulated = jnp.zeros((n_heads, TABLE_LANES), F32)
-
-        def table_step(i, acc):
-            line = dscore[:, pl.ds(i, 1), :].reshape(n_heads, SLOT)
-            high = line.astype(BF16)
-            rest = line - high.astype(F32)
-            middle = rest.astype(BF16)
-            least = (rest - middle.astype(F32)).astype(BF16)
-            three = jnp.concatenate([high, middle, least], axis=0)
-            out = dot(three, hot_ref[i])
-            return acc + ((out[2 * n_heads :] + out[n_heads : 2 * n_heads]) + out[:n_heads])
-
-        accumulated = lax.fori_loop(0, WIN * WIN, table_step, accumulated)
-        hl = n_heads // 2
-        small[l, 16 : 16 + hl, 0:TABLE_LANES] = accumulated[:hl]
-        small[l, 16 : 16 + hl, TABLE_LANES : 2 * TABLE_LANES] = accumulated[hl:]
-
     lows = [(low.at[n], spill_small.at[n]) for n in range(5)]
     moves = {
         "ain": [lows[X1], lows[AIN]], "mix": [lows[MIX], lows[X2], lows[FIN]],
@@ -1046,34 +1107,46 @@
     pl.semaphore_wait(barrier, Z - 1 + 3)
     ag((0, 0), 1)
     begin(small_in)
-    for c in range(1, len(plan.gather_chunks)):
-        ag((0, c), 1)
     for l in range(L):
         W[l, t, z, y, x] = shard_ref[l]
     small[...] = jnp.zeros_like(small)
 
-    for stage in (2, 3, 4):
-        push(ag, (0, 0), stage)
+    gap(1)
+    push(ag, (0, 0), 2)
+    push(ag, (0, 1), 1)
+    push(ag, (0, 0), 3)
+    gap(3)
+    push(ag, (0, 0), 4)
+    push(ag, (0, 2), 1)
     push(ag, (0, 0), 5, mark=(0, 0))
     push(ag, (0, 1), 2)
+    gap(3)
+    push(ag, (0, 1), 3)
     push(ag, (0, 2), 2)
-    push(ag, (0, 1), 3)
-    for c in range(3):
-        push(ag, (1, c), 1)
+    push(ag, (1, 0), 1)
+    gap(11)
+    push(ag, (0, 1), 4)
     push(ag, (0, 2), 3)
-    push(ag, (0, 1), 4)
+    push(ag, (0, 1), 5, mark=(0, 1))
+    push(ag, (1, 1), 1)
+    gap(1)
     push(ag, (0, 2), 4)
-    push(ag, (0, 1), 5, mark=(0, 1))
     push(ag, (1, 0), 2)
+    push(ag, (1, 0), 3)
+    push(ag, (1, 2), 1)
+    gap(1)
+    push(ag, (1, 0), 4)
+    push(ag, (0, 2), 5, mark=(0, 2))
     push(ag, (1, 1), 2)
-    push(ag, (0, 2), 5, mark=(0, 2))
-    push(ag, (1, 0), 3)
+    gap(2)
+    push(ag, (1, 1), 3)
+    push(ag, (1, 0), 5, mark=(1, 0))
+    push(ag, (1, 1), 4)
     push(ag, (1, 2), 2)
-    push(ag, (1, 1), 3)
-    push(ag, (1, 0), 4)
+    gap(2)
+    gap(2)
     push(ag, (1, 2), 3)
-    push(ag, (1, 1), 4)
-    push(ag, (1, 0), 5, mark=(1, 0))
+    gap(10)
     push(ag, (1, 2), 4)
     push(ag, (1, 1), 5, mark=(1, 1))
     push(ag, (1, 2), 5, mark=(1, 2))
@@ -1144,13 +1217,14 @@
     tab = jnp.pad(bias_table.astype(F32), ((0, 0), (0, 0), (0, TABLE_LANES - TABLE)))
     params = jnp.stack([norm1_gain, norm1_bias, proj_bias, norm2_gain, norm2_bias, fc2_bias], axis=1).astype(F32)
     params = jnp.pad(params, ((0, 0), (0, 2), (0, 0)))
-    index_padded = jnp.pad(rel_index, ((0, pad), (0, pad)), constant_values=-1)
+    index_padded = jnp.pad(rel_index.T, ((0, pad), (0, pad)), constant_values=-1)
     hot = (index_padded[:, :, None] == jnp.arange(TABLE_LANES, dtype=jnp.int32)).astype(BF16)
     regions = region_ids.reshape(plan.windows, win_tokens)
     shift_mask = jnp.where(regions[:, :, None] == regions[:, None, :], 0.0, MASKED).astype(F32)
-    mask = jnp.stack([jnp.zeros_like(shift_mask), shift_mask])
-    mask = jnp.pad(mask, ((0, 0), (0, 0), (0, pad), (0, 0)))
-    mask = jnp.pad(mask, ((0, 0), (0, 0), (0, 0), (0, pad)), constant_values=PADDED)
+    mask = jnp.concatenate([jnp.zeros_like(shift_mask[:1]), shift_mask], axis=0)
+    mask = jnp.pad(mask, ((0, 0), (0, 0), (0, pad)))
+    mask = jnp.pad(mask, ((0, 0), (0, pad), (0, 0)), constant_values=PADDED)
+    mask = jnp.tile(mask, (1, 1, PACK))
 
     vmem = pl.BlockSpec(memory_space=pltpu.VMEM)
     anywhere = pl.BlockSpec(memory_space=pl.ANY)
@@ -1181,8 +1255,8 @@
             pltpu.VMEM((M, 3 * width), BF16),
             pltpu.VMEM((M, width), BF16),
             pltpu.VMEM((M, width), F32),
-            pltpu.VMEM((L, T * hl, SLOT, SLOT), F32),
-            pltpu.VMEM((T * hl, SLOT, SLOT), F32),
+            pltpu.VMEM(((plan.windows + 1) * plan.groups, SLOT, PACK * SLOT), F32),
+            pltpu.VMEM((8, SLOT, PACK * SLOT), F32),
             pltpu.VMEM((2, 8, width), F32),
             pltpu.VMEM((L, SMALL_ROWS, width), F32),
             pltpu.VMEM((4, L, SMALL_ROWS, width), F32),
@@ -1212,7 +1286,9 @@
     qv_total = lax.dynamic_slice_in_dim(total[:, 6:8], t_index * local, local, 2)
     fc1_total = total[:, 8 : 8 + T * ffl // width].reshape(L, T * ffl)
     fc1_total = lax.dynamic_slice_in_dim(fc1_total, t_index * ffl, ffl, 1)
-    table_total = lax.dynamic_slice_in_dim(total[:, 16 : 16 + hl], t_index * TABLE_LANES, TABLE_LANES, 2)[..., :TABLE]
+    table_total = total[:, 16 : 16 + 2 * plan.groups].reshape(L, 2, plan.groups, PACK // 2, TABLE_LANES)
+    table_total = table_total.transpose(0, 2, 3, 1, 4).reshape(L, T * hl, TABLE_LANES)
+    table_total = lax.dynamic_slice_in_dim(table_total, t_index * hl, hl, 1)[..., :TABLE]
     a, b, c = 3 * local, 4 * local, 4 * local + ffl
     return (
         unpadded(out), unpadded(g_in), total[:, 0], total[:, 1],
@@ -1233,7 +1309,7 @@
     heads_local = bias_table.shape[1]
     return (
         n_t == 2 and n_dp % 4 == 0 and z >= 2 and z & (z - 1) == 0
-        and heads_local * HD % LANES == 0 and heads_local % 8 == 0 and heads_local <= 8
+        and heads_local * HD % LANES == 0 and heads_local == 2 * LANES // HD and LAYERS == 2
         and width // n_dp % 16 == 0 and width == 2 * TABLE_LANES and fc1_bias.shape[1] % width == 0
         and 8 + 2 * fc1_bias.shape[1] // width <= 16
         and tokens % (GRID * GRID) == 0 and tokens <= 4 * GRID * GRID

time: 382 us -> 276 us (0.72)
  Pallas kernels: 348 us -> 241 us
    pallas_call x1, Pallas kernels: 348 us -> 241 us  [fast_device(): pl.pallas_call(functools.partial(step_kernel, plan), out_shape=(jax.Shape...]
where the time goes in v1:
time: 276 us
  Pallas kernels  241 us (87%)
  local copies, waits for them, and re-layouts  29.3 us (11%)
  other arithmetic  4.55 us (2%)
    pallas_call x1, Pallas kernels, fast_device(): pl.pallas_call(functools.partial(step_kernel, plan), out_shape=(jax.Shape...  241 us
    unnamed x37, local copies, waits for them, and re-layouts  6.06 us

profile of v1, /device:TPU:0, one launch (start us, length us, event | category | flops | bytes accessed | tf_op | source)
XLA Modules:
  0.0 275.6 jit_solution(4554173057947673406)
XLA Ops:
  0.7 0.8 slice_bitcast_fusion.7
  1.5 0.9 slice_bitcast_fusion.5
  2.4 1.0 slice_bitcast_fusion.4
  3.4 0.7 slice_bitcast_fusion.10
  4.1 0.9 pad_maximum_fusion.refs_2_
  5.1 1.7 fusion.refs_7_
  7.0 1.1 pad.40
  8.5 1.1 pad.41
  9.9 1.2 tile.10.refs_6_
  11.1 0.6 pad_convert_fusion
  11.7 1.5 scatter.14.refs_3_
  14.6 240.8 %whole_step.1 = (f32[1024,512]{1,0:T(8,128)}, f32[1024,512]{1,0:T(8,128)}, f32[2,32,3072]{2,1,0:T(8,128)}, f32[2,24,512]{2,1,0:T(8,128)}, bf16[2,1024,2048]{2,1,...) custom-call(bf16[1024,512]{1,0:T(8,128)(2,1)} %bitcast.75, ...), custom_call_target="tpu_custom_call" | custom-call | tf_op jit(solution)/shard_map/whole_step/pallas_call | solution.py:1233
  255.4 0.8 slice.133
  256.9 0.8 slice_bitcast_fusion.8
  258.3 0.8 slice.132
  259.6 1.1 fusion.1
  264.3 1.9 slice_bitcast_fusion
  266.2 0.9 slice.131
  267.2 0.7 copy.48
  267.9 1.5 slice_bitcast_fusion.1
  269.4 1.7 slice.143
  271.1 1.4 reshape.159
  272.5 1.7 slice.144
  274.2 1.4 reshape.161
  (62 shorter events, 7.9 us)
Async XLA Ops:
  0.6 4.4 %copy-start.2 = (s32[49,49]{1,0:T(8,128)S(1)}, s32[49,49]{1,0:T(8,128)}, u32[]{:S(2)}) copy-start(s32[49,49]{1,0:T(8,128)} %param.24) | copy-start | bytes 28816
  2.4 4.4 %copy-start = (bf16[784,512]{1,0:T(8,128)(2,1)S(1)}, bf16[784,512]{1,0:T(8,128)(2,1)}, u32[]{:S(2)}) copy-start(bf16[784,512]{1,0:T(8,128)(2,1)} %param.21) | copy-start | bytes 2408452
  6.8 1.4 copy-start.1
  8.1 1.5 copy-start.12
  8.4 2.7 copy-start.4
  8.4 3.3 %copy-start.5 = (bf16[2,2,256]{2,1,0:T(2,128)(2,1)S(1)}, bf16[2,2,256]{2,1,0:T(2,128)(2,1)}, u32[]{:S(2)}) copy-start(bf16[2,2,256]{2,1,0:T(2,128)(2,1)} %param.28) | copy-start | bytes 6148
  8.4 4.8 %copy-start.6 = (bf16[2,512]{1,0:T(2,128)(2,1)S(1)}, bf16[2,512]{1,0:T(2,128)(2,1)}, u32[]{:S(2)}) copy-start(bf16[2,512]{1,0:T(2,128)(2,1)} %param.25) | copy-start | bytes 6148
  8.4 4.8 %copy-start.7 = (bf16[2,512]{1,0:T(2,128)(2,1)S(1)}, bf16[2,512]{1,0:T(2,128)(2,1)}, u32[]{:S(2)}) copy-start(bf16[2,512]{1,0:T(2,128)(2,1)} %param.26) | copy-start | bytes 6148
  8.4 4.8 %copy-start.8 = (bf16[2,512]{1,0:T(2,128)(2,1)S(1)}, bf16[2,512]{1,0:T(2,128)(2,1)}, u32[]{:S(2)}) copy-start(bf16[2,512]{1,0:T(2,128)(2,1)} %param.31) | copy-start | bytes 6148
  8.5 4.8 %copy-start.9 = (bf16[2,512]{1,0:T(2,128)(2,1)S(1)}, bf16[2,512]{1,0:T(2,128)(2,1)}, u32[]{:S(2)}) copy-start(bf16[2,512]{1,0:T(2,128)(2,1)} %param.32) | copy-start | bytes 6148
  8.5 4.8 %copy-start.10 = (bf16[2,512]{1,0:T(2,128)(2,1)S(1)}, bf16[2,512]{1,0:T(2,128)(2,1)}, u32[]{:S(2)}) copy-start(bf16[2,512]{1,0:T(2,128)(2,1)} %param.33) | copy-start | bytes 6148
  8.5 4.8 %copy-start.11 = (bf16[2,512]{1,0:T(2,128)(2,1)S(1)}, bf16[2,512]{1,0:T(2,128)(2,1)}, u32[]{:S(2)}) copy-start(bf16[2,512]{1,0:T(2,128)(2,1)} %param.37) | copy-start | bytes 6148
  8.5 5.5 %copy-start.3 = (bf16[2,8,169]{2,1,0:T(8,128)(2,1)S(1)}, bf16[2,8,169]{2,1,0:T(8,128)(2,1)}, u32[]{:S(2)}) copy-start(bf16[2,8,169]{2,1,0:T(8,128)(2,1)} %param.29) | copy-start | bytes 16228
